TPU v7x, 32 devices: a whole 2x2x4 slice. The times are simulated.
32 devices in a mesh: groups: 2 (over x), shard: 16 (over z, y, core).
Axes of the slice: x: 2, y: 2, z: 4, core: 2. Of those that a mesh axis runs over, the one named last changes fastest.
Arguments:
- hidden: bfloat16 [8192, 2048], P(('groups', 'shard')), parts along dimension 0, may hold values from -10 to 10
- query_rows: bfloat16 [8192, 4096], P(('groups', 'shard')), parts along dimension 0, may hold values from -9 to 9
- key_rows: bfloat16 [8192, 512], P(('groups', 'shard')), parts along dimension 0, may hold values from -9 to 9
- value_rows: bfloat16 [8192, 512], P(('groups', 'shard')), parts along dimension 0, may hold values from -6 to 6
- counts: int32 [2], P('groups'), parts along dimension 0, may hold values from 1024 to 4096
- out_weight: bfloat16 [4096, 2048], P('shard'), may hold values from -0.09375 to 0.09375
- norm_gain: bfloat16 [2048], replicated, may hold values from 0.099609375 to 1.8984375
- route_ids: int32 [8192, 8], P(('groups', 'shard')), parts along dimension 0, may hold values from 0 to 31, all different within a row; in each aligned block of 256 rows (0 to 255, 256 to 511, ...) at most 80 rows name the same one
- route_weights: bfloat16 [8192, 8], P(('groups', 'shard')), parts along dimension 0, may hold values from 0.099609375 to 0.3984375
- w_gate: bfloat16 [32, 2048, 768], P('shard'), may hold values from -0.125 to 0.125
- w_up: bfloat16 [32, 2048, 768], P('shard'), may hold values from -0.125 to 0.125
- w_down: bfloat16 [32, 768, 2048], P('shard'), may hold values from -0.21875 to 0.21875
Outputs:
- layer_out: bfloat16 [8192, 2048], P(('groups', 'shard')), parts along dimension 0
There are 2 independent parts, one for each index of `groups`. A program takes and returns all parts, laid end to end along the dimension named above; an argument that names none is the same for every part. Nothing has to cross between parts.
Inputs may be any that keep to these rules, and one draw needn't show every extreme that they name: `route_ids`: each row names 8 different experts; in the rows of one device no expert is named by more than 80 rows, a bound that some block reaches.
All inputs are finite; a program needn't handle non-finite values.
Results may differ from a plain program's by a relative error of at most 0.008.
Values may be sent and summed in bfloat16 or wider, within the bound.
A program may use at most 384 MiB of HBM per device.

v0:
```python
import functools
import math

import jax
import jax.numpy as jnp
from jax import lax
from jax.experimental import pallas as pl
from jax.experimental.pallas import tpu as pltpu
from jax.sharding import PartitionSpec as P

HD = 128
SEQ_LEN = 4096
NEG = -1e30
MESH = pl.DeviceIdType.MESH


def ring_place(chips, index):
    if chips == 8:
        z, y = index // 2, index % 2
        return z + y * (7 - 2 * z)
    return index


def ring_chip(chips, place):
    if chips == 8:
        half = place // 4
        z = place + half * (7 - 2 * place)
        return 2 * z + half
    return place


def gather_kernel(devices, pieces, x_ref, o_ref, local_sem, near_send, near_recv, send, recv):
    chips = devices // 2
    me = lax.axis_index("shard")
    group = lax.axis_index("groups")
    core = me % 2
    place = ring_place(chips, me // 2)

    def device_at(offset):
        return ring_chip(chips, (place + offset + 2 * chips) % chips) * 2 + core

    right, left, sibling = device_at(1), device_at(-1), me + 1 - 2 * core
    barrier = pltpu.get_barrier_semaphore()
    for other in (right, left, sibling):
        pl.semaphore_signal(barrier, inc=1, device_id=(group, other), device_id_type=MESH)
    pl.semaphore_wait(barrier, 3)

    rows = x_ref.shape[0] // (2 * pieces)

    def part(ref, way, piece):
        return ref.at[pl.ds((way * pieces + piece) * rows, rows)]

    def hop(step, way, piece):
        origin = device_at(-step if way == 0 else step)
        src = part(x_ref if step == 0 else o_ref.at[origin], way, piece)
        return pltpu.make_async_remote_copy(
            src_ref=src,
            dst_ref=part(o_ref.at[origin], way, piece),
            send_sem=send.at[step, way, piece],
            recv_sem=recv.at[step, way, piece],
            device_id=(group, right if way == 0 else left),
            device_id_type=MESH,
        )

    def landing(step, way, piece):
        origin = device_at(-step - 1 if way == 0 else step + 1)
        place_of = part(o_ref.at[origin], way, piece)
        return pltpu.make_async_remote_copy(
            src_ref=place_of,
            dst_ref=place_of,
            send_sem=send.at[step, way, piece],
            recv_sem=recv.at[step, way, piece],
            device_id=(group, right if way == 0 else left),
            device_id_type=MESH,
        )

    def near(step, way, piece):
        if step < 0:
            src, origin = part(x_ref, way, piece), me
        else:
            origin = device_at(-step - 1 if way == 0 else step + 1)
            src = part(o_ref.at[origin], way, piece)
        return pltpu.make_async_remote_copy(
            src_ref=src,
            dst_ref=part(o_ref.at[origin], way, piece),
            send_sem=near_send.at[step + 1, way, piece],
            recv_sem=near_recv.at[step + 1, way, piece],
            device_id=(group, sibling),
            device_id_type=MESH,
        )

    def near_landing(step, way, piece):
        if step < 0:
            origin = sibling
        else:
            origin = device_at(-step - 1 if way == 0 else step + 1) + 1 - 2 * core
        place_of = part(o_ref.at[origin], way, piece)
        return pltpu.make_async_remote_copy(
            src_ref=place_of,
            dst_ref=place_of,
            send_sem=near_send.at[step + 1, way, piece],
            recv_sem=near_recv.at[step + 1, way, piece],
            device_id=(group, sibling),
            device_id_type=MESH,
        )

    every = [(way, piece) for piece in range(pieces) for way in range(2)]
    for way, piece in every:
        hop(0, way, piece).start()
    own = pltpu.make_async_copy(x_ref, o_ref.at[me], local_sem)
    own.start()
    for way, piece in every:
        near(-1, way, piece).start()
    for step in range(chips - 1):
        for way, piece in every:
            landing(step, way, piece).wait_recv()
            if step + 1 < chips - 1:
                hop(step + 1, way, piece).start()
            near(step, way, piece).start()
    own.wait()
    for step in range(chips - 1):
        for way, piece in every:
            hop(step, way, piece).wait_send()
    for step in range(-1, chips - 1):
        for way, piece in every:
            near(step, way, piece).wait_send()
            near_landing(step, way, piece).wait_recv()


def ring_gather(x, devices, collective_id, pieces=2):
    steps = devices // 2
    dma = pltpu.SemaphoreType.DMA
    return pl.pallas_call(
        functools.partial(gather_kernel, devices, pieces),
        out_shape=jax.ShapeDtypeStruct((devices,) + x.shape, x.dtype),
        in_specs=[pl.BlockSpec(memory_space=pltpu.HBM)],
        out_specs=pl.BlockSpec(memory_space=pltpu.HBM),
        scratch_shapes=[
            dma,
            dma((steps, 2, pieces)),
            dma((steps, 2, pieces)),
            dma((steps, 2, pieces)),
            dma((steps, 2, pieces)),
        ],
        compiler_params=pltpu.CompilerParams(collective_id=collective_id, has_side_effects=True),
    )(x)


def scatter_kernel(
    devices, pieces, x_ref, o_ref, held, near_in, ring_in, load, near_send, near_recv, send, recv
):
    chips = devices // 2
    me = lax.axis_index("shard")
    group = lax.axis_index("groups")
    core = me % 2
    place = ring_place(chips, me // 2)

    def chip_at(offset):
        return ring_chip(chips, (place + offset + 2 * chips) % chips) * 2

    right, left, sibling = chip_at(1) + core, chip_at(-1) + core, me + 1 - 2 * core
    barrier = pltpu.get_barrier_semaphore()
    for other in (right, left, sibling):
        pl.semaphore_signal(barrier, inc=1, device_id=(group, other), device_id_type=MESH)
    pl.semaphore_wait(barrier, 3)

    rows = x_ref.shape[1] // (2 * pieces)
    every = [(way, piece) for piece in range(pieces) for way in range(2)]

    def span(way, piece):
        return pl.ds((way * pieces + piece) * rows, rows)

    def target(step, way):
        return chip_at(-step - 1 if way == 0 else step + 1)

    def fetch(step, way, piece):
        return pltpu.make_async_copy(
            x_ref.at[target(step, way) + core, span(way, piece)],
            held.at[step, span(way, piece)],
            load.at[step, way, piece],
        )

    def near(step, way, piece):
        return pltpu.make_async_remote_copy(
            src_ref=x_ref.at[target(step, way) + 1 - core, span(way, piece)],
            dst_ref=near_in.at[step, span(way, piece)],
            send_sem=near_send.at[step, way, piece],
            recv_sem=near_recv.at[step, way, piece],
            device_id=(group, sibling),
            device_id_type=MESH,
        )

    def hop(step, way, piece):
        return pltpu.make_async_remote_copy(
            src_ref=held.at[step, span(way, piece)],
            dst_ref=ring_in.at[step, span(way, piece)],
            send_sem=send.at[step, way, piece],
            recv_sem=recv.at[step, way, piece],
            device_id=(group, right if way == 0 else left),
            device_id_type=MESH,
        )

    for step in range(chips):
        for way, piece in every:
            near(step, way, piece).start()
            fetch(step, way, piece).start()
    for step in range(chips):
        for way, piece in every:
            here = span(way, piece)
            fetch(step, way, piece).wait()
            near(step, way, piece).wait_recv()
            total = held[step, here, :].astype(jnp.float32) + near_in[step, here, :].astype(
                jnp.float32
            )
            if step > 0:
                hop(step - 1, way, piece).wait_recv()
                total = total + ring_in[step - 1, here, :].astype(jnp.float32)
            if step < chips - 1:
                held[step, here, :] = total.astype(held.dtype)
                hop(step, way, piece).start()
            else:
                o_ref[here, :] = total.astype(o_ref.dtype)
    for step in range(chips):
        for way, piece in every:
            near(step, way, piece).wait_send()
            if step < chips - 1:
                hop(step, way, piece).wait_send()


def ring_scatter(x, collective_id, pieces=2):
    devices, rows, depth = x.shape
    chips = devices // 2
    dma = pltpu.SemaphoreType.DMA
    sems = dma((chips, 2, pieces))
    return pl.pallas_call(
        functools.partial(scatter_kernel, devices, pieces),
        out_shape=jax.ShapeDtypeStruct((rows, depth), x.dtype),
        in_specs=[pl.BlockSpec(memory_space=pltpu.HBM)],
        out_specs=pl.BlockSpec(memory_space=pltpu.VMEM),
        scratch_shapes=[pltpu.VMEM((chips, rows, depth), x.dtype)] * 2
        + [pltpu.VMEM((chips - 1, rows, depth), x.dtype)]
        + [sems] * 5,
        compiler_params=pltpu.CompilerParams(
            collective_id=collective_id, has_side_effects=True, vmem_limit_bytes=40 << 20
        ),
    )(x)


def attend_kernel(step_rows, heads, count_ref, first_ref, q_ref, k_ref, v_ref, o_ref, qs, top, total):
    rows = q_ref.shape[0]
    scale = math.log2(math.e) / math.sqrt(HD)
    count = count_ref[0]
    first = first_ref[0]
    seen = jnp.minimum(count, first + rows)
    blocks = jnp.where(first < count, (seen + step_rows - 1) // step_rows, 0)
    for h in range(heads):
        qs[h * rows : (h + 1) * rows, :] = q_ref[:, h * HD : (h + 1) * HD]
    top[...] = jnp.full(top.shape, NEG, jnp.float32)
    total[...] = jnp.zeros(total.shape, jnp.float32)
    ones = jnp.ones((step_rows, HD), jnp.bfloat16)

    def fold(start, masked):
        start = pl.multiple_of(start, step_rows)
        keys = k_ref[pl.ds(start, step_rows), :]
        values = jnp.concatenate([v_ref[pl.ds(start, step_rows), :], ones], axis=1)
        if masked:
            at_row = first + lax.broadcasted_iota(jnp.int32, (rows, step_rows), 0)
            at_col = start + lax.broadcasted_iota(jnp.int32, (rows, step_rows), 1)
            visible = (at_col <= at_row) & (at_col < count)
        for h in range(heads):
            span = slice(h * rows, (h + 1) * rows)
            scores = lax.dot_general(
                qs[span, :], keys, (((1,), (1,)), ((), ())), preferred_element_type=jnp.float32
            )
            if masked:
                scores = jnp.where(visible, scores, NEG)
            old = top[span, :]
            new = jnp.maximum(old, jnp.max(scores, axis=1, keepdims=True) * scale)
            expo = jnp.exp2(scores * scale - new[:, :1]).astype(jnp.bfloat16)
            factor = jnp.exp2(old - new)
            part = jnp.dot(expo, values, preferred_element_type=jnp.float32)
            total[span, :] = total[span, :] * jnp.concatenate([factor, factor], axis=1) + part
            top[span, :] = new

    def body(i, carry):
        fold(i * step_rows, False)
        return carry

    lax.fori_loop(0, blocks - 1, body, 0)

    @pl.when(blocks > 0)
    def _():
        fold((blocks - 1) * step_rows, True)

    live = first + lax.broadcasted_iota(jnp.int32, (rows, HD), 0) < count
    for h in range(heads):
        both = total[h * rows : (h + 1) * rows, :]
        result = jnp.where(live, both[:, :HD] / jnp.where(live, both[:, HD:], 1.0), 0.0)
        o_ref[:, h * HD : (h + 1) * HD] = result.astype(jnp.bfloat16)


def attend(count, first, queries, keys_values, kv_count):
    rows, width = queries.shape
    length = keys_values.shape[0]
    heads = width // HD // kv_count
    step_rows = math.gcd(length, 512)
    smem = pl.BlockSpec(memory_space=pltpu.SMEM)
    return pl.pallas_call(
        functools.partial(attend_kernel, step_rows, heads),
        grid=(kv_count,),
        out_shape=jax.ShapeDtypeStruct((rows, width), jnp.bfloat16),
        in_specs=[
            smem,
            smem,
            pl.BlockSpec((rows, heads * HD), lambda g: (0, g)),
            pl.BlockSpec((length, HD), lambda g: (0, g)),
            pl.BlockSpec((length, HD), lambda g: (0, kv_count + g)),
        ],
        out_specs=pl.BlockSpec((rows, heads * HD), lambda g: (0, g)),
        scratch_shapes=[
            pltpu.VMEM((heads * rows, HD), jnp.bfloat16),
            pltpu.VMEM((heads * rows, HD), jnp.float32),
            pltpu.VMEM((heads * rows, 2 * HD), jnp.float32),
        ],
        compiler_params=pltpu.CompilerParams(vmem_limit_bytes=40 << 20),
        cost_estimate=pl.CostEstimate(
            flops=4 * rows * width * length, bytes_accessed=12 << 20, transcendentals=rows * width * length // HD
        ),
    )(count, first, queries, keys_values, keys_values)


def expert_kernel(local, cap, per, count_ref, x_ref, info_ref, wg_ref, wu_ref, wd_ref, o_ref, picked, given):
    rows = x_ref.shape[1]
    start = pl.program_id(0) * per * rows
    alive = start % SEQ_LEN < count_ref[0]

    @pl.when(jnp.logical_not(alive))
    def _():
        o_ref[...] = jnp.zeros(o_ref.shape, o_ref.dtype)

    @pl.when(alive)
    def _():
        before = (
            lax.broadcasted_iota(jnp.int32, (rows, rows), 0)
            < lax.broadcasted_iota(jnp.int32, (rows, rows), 1)
        ).astype(jnp.bfloat16)
        slot_at = lax.broadcasted_iota(jnp.int32, (cap, rows), 0).astype(jnp.float32)
        choices = []
        weights = [[] for _ in range(local)]
        for b in range(per):
            info = info_ref[b]
            slots = jnp.dot(info.astype(jnp.bfloat16), before, preferred_element_type=jnp.float32)
            mine = []
            for e in range(local):
                hit = (slot_at == slots[e : e + 1]) & (info[e : e + 1] > 0.5)
                mine.append(jnp.where(hit, 1.0, 0.0))
                weights[e].append(
                    jnp.sum(
                        jnp.where(hit, info[local + e : local + e + 1], 0.0), axis=1, keepdims=True
                    )
                )
            choice = jnp.concatenate(mine, axis=0).astype(jnp.bfloat16)
            choices.append(choice)
            rows_here = jnp.dot(choice, x_ref[b], preferred_element_type=jnp.float32)
            rows_here = rows_here.astype(jnp.bfloat16)
            for e in range(local):
                picked[e, b * cap : (b + 1) * cap, :] = rows_here[e * cap : (e + 1) * cap]
        for e in range(local):
            mine = picked[e]
            gate = jnp.dot(mine, wg_ref[e], preferred_element_type=jnp.float32)
            up = jnp.dot(mine, wu_ref[e], preferred_element_type=jnp.float32)
            act = (gate / (1.0 + jnp.exp(-gate)) * up).astype(jnp.bfloat16)
            down = jnp.dot(act, wd_ref[e], preferred_element_type=jnp.float32)
            down = (down * jnp.concatenate(weights[e], axis=0)).astype(jnp.bfloat16)
            for b in range(per):
                given[b, e * cap : (e + 1) * cap, :] = down[b * cap : (b + 1) * cap]
        for b in range(per):
            back = lax.dot_general(
                choices[b], given[b], (((0,), (0,)), ((), ())), preferred_element_type=jnp.float32
            )
            o_ref[b] = back.astype(o_ref.dtype)


def expert_sums(count, rows_all, info, w_gate, w_up, w_down, cap):
    devices, rows, depth = rows_all.shape
    local, _, hidden_units = w_gate.shape
    per = 4
    whole = pl.Buffered(1)
    return pl.pallas_call(
        functools.partial(expert_kernel, local, cap, per),
        grid=(devices // per,),
        out_shape=jax.ShapeDtypeStruct((devices, rows, depth), jnp.bfloat16),
        in_specs=[
            pl.BlockSpec(memory_space=pltpu.SMEM),
            pl.BlockSpec((per, rows, depth), lambda i: (i, 0, 0)),
            pl.BlockSpec((per,) + info.shape[1:], lambda i: (i, 0, 0)),
            pl.BlockSpec(w_gate.shape, lambda i: (0, 0, 0), pipeline_mode=whole),
            pl.BlockSpec(w_up.shape, lambda i: (0, 0, 0), pipeline_mode=whole),
            pl.BlockSpec(w_down.shape, lambda i: (0, 0, 0), pipeline_mode=whole),
        ],
        out_specs=pl.BlockSpec((per, rows, depth), lambda i: (i, 0, 0)),
        scratch_shapes=[
            pltpu.VMEM((local, per * cap, depth), jnp.bfloat16),
            pltpu.VMEM((per, local * cap, depth), jnp.bfloat16),
        ],
        compiler_params=pltpu.CompilerParams(vmem_limit_bytes=60 << 20),
    )(count, rows_all, info, w_gate, w_up, w_down)


def per_device(
    hidden,
    query_rows,
    key_rows,
    value_rows,
    counts,
    out_weight,
    norm_gain,
    route_ids,
    route_weights,
    w_gate,
    w_up,
    w_down,
):
    devices = lax.axis_size("shard")
    me = lax.axis_index("shard")
    tok_dev, depth = hidden.shape
    topk = route_ids.shape[1]
    local = w_gate.shape[0]
    experts = local * devices
    capacity = max(2, tok_dev * topk * 5 // (4 * experts))
    capacity = -(-capacity // 16) * 16

    kv_width = 2 * key_rows.shape[1]
    routing = jnp.concatenate([route_ids.astype(jnp.bfloat16), route_weights], axis=1)
    routing = jnp.pad(routing, ((0, 0), (0, HD - 2 * topk)))
    both = ring_gather(jnp.concatenate([key_rows, value_rows, routing], axis=1), devices, 0)
    ids_all = both[:, :, kv_width : kv_width + topk].astype(jnp.int32)
    weights_all = both[:, :, kv_width + topk : kv_width + 2 * topk]
    live_all = jnp.arange(devices * tok_dev, dtype=jnp.int32).reshape(devices, tok_dev) < counts[0]
    info = []
    for e in range(local):
        info.append(jnp.sum((ids_all == me * local + e).astype(jnp.float32), axis=2))
    for e in range(local):
        matched = jnp.where(ids_all == me * local + e, weights_all.astype(jnp.float32), 0.0)
        info.append(jnp.where(live_all, jnp.sum(matched, axis=2), 0.0))
    info = jnp.stack(info, axis=1)
    info = jnp.pad(info, ((0, 0), (0, -info.shape[1] % 8), (0, 0)))

    both = both.reshape(devices * tok_dev, both.shape[2])
    first = (me * tok_dev).astype(jnp.int32).reshape(1)
    attended = attend(counts, first, query_rows, both, key_rows.shape[1] // HD)
    out_all = ring_gather(out_weight, devices, 1).reshape(-1, depth)
    mixed_rows = hidden.astype(jnp.float32) + jnp.dot(
        attended, out_all, preferred_element_type=jnp.float32
    )
    mean_square = jnp.mean(mixed_rows * mixed_rows, axis=1, keepdims=True)
    normed = (mixed_rows * lax.rsqrt(mean_square + 1e-06) * norm_gain.astype(jnp.float32)).astype(
        jnp.bfloat16
    )
    normed_all = ring_gather(normed, devices, 2)
    sums = expert_sums(counts, normed_all, info, w_gate, w_up, w_down, capacity)
    summed = ring_scatter(sums, 3)
    return (mixed_rows + summed.astype(jnp.float32)).astype(jnp.bfloat16)


def solution(mesh):
    rows = P(("groups", "shard"), None)
    weights = P("shard", None, None)
    return jax.shard_map(
        per_device,
        mesh=mesh,
        in_specs=(
            rows,
            rows,
            rows,
            rows,
            P("groups"),
            P("shard", None),
            P(),
            rows,
            rows,
            weights,
            weights,
            weights,
        ),
        out_specs=rows,
        check_vma=False,
    )
```

profile of v0, /device:TPU:3, one launch (start us, length us, event | category | flops | bytes accessed | tf_op | source)
XLA Modules:
  0.0 452.6 jit_solution(13087746378965696634)
XLA Ops:
  0.7 0.7 convert_element_type.36
  1.4 0.7 pad_maximum_fusion
  2.0 0.7 convert_element_type.37
  2.7 0.1 copy.15
  2.9 1.9 fusion.3.x_ref
  4.7 51.4 %shard_map.118 = bf16[16,256,1152]{2,1,0:T(8,128)(2,1)} custom-call(bf16[256,1152]{1,0:T(8,128)(2,1)} %fusion.3.x_ref), custom_call_target="tpu_custom_call" | custom-call | tf_op jit(solution)/shard_map/pallas_call | solution.py:133
  56.1 0.0 copy-start.1
  56.1 4.0 convert_reduce_fusion.1
  60.2 0.7 select_maximum_fusion.info_ref
  60.9 0.0 copy-done.1
  60.9 0.0 copy-start
  60.9 3.7 copy-done
  64.6 13.1 %shard_map.119 = bf16[256,4096]{1,0:T(8,128)(2,1)S(1)} custom-call(s32[1]{0:T(128)} %copy.16.count_ref, s32[1]{0:T(128)} %bitcast.first_ref, bf16[256,4096]{1,0:T(8,128)(2,1)S(1)} %copy-done.1, bf16[4096,1152]{1,0:T(8,128)(2,1)S(1)} %bitcast.7, bf16[4096,1152]{1,0:T(8,128)(2,1)S(1)} %bitcast.8), custom_call_target="tpu_custom_call" | custom-call | flops 17179869184 | bytes 12582912 | tf_op jit(solution)/shard_map/pallas_call | solution.py:308
  77.7 0.0 copy-start.4
  77.7 136.6 %shard_map.120 = bf16[16,256,2048]{2,1,0:T(8,128)(2,1)} custom-call(bf16[256,2048]{1,0:T(8,128)(2,1)} %x_ref.1), custom_call_target="tpu_custom_call" | custom-call | tf_op jit(solution)/shard_map/pallas_call | solution.py:133
  214.3 0.0 copy-done.4
  214.3 8.3 %multiply_reduce_fusion = (f32[256]{0:T(256)S(1)}, f32[256,2048]{1,0:T(8,128)S(1)}) fusion(bf16[256,4096]{1,0:T(8,128)(2,1)S(1)} %shard_map.119, bf16[4096,2048]{1,0:T(8,128)(2,1)} %bitcast.9, bf16[256,2048]{1,0:T(8,128)(2,1)S(1)} %copy-done.4), kind=kOutput, calls=%fused_computation.11 | convolution fusion | flops 4297064448 | bytes 22021120 | tf_op jit(solution)/shard_map/dot_general | solution.py:453
  222.6 0.0 copy-start.2
  222.6 1.3 copy-done.2
  223.9 1.2 multiply_convert_fusion.x_ref
  225.1 94.2 %shard_map.121.x_ref = bf16[16,256,2048]{2,1,0:T(8,128)(2,1)} custom-call(bf16[256,2048]{1,0:T(8,128)(2,1)} %multiply_convert_fusion.x_ref), custom_call_target="tpu_custom_call" | custom-call | tf_op jit(solution)/shard_map/pallas_call | solution.py:133
  319.3 44.5 %shard_map.122.x_ref = bf16[16,256,2048]{2,1,0:T(8,128)(2,1)} custom-call(s32[1]{0:T(128)} %copy.16.count_ref, bf16[16,256,2048]{2,1,0:T(8,128)(2,1)} %shard_map.121.x_ref, f32[16,8,256]{2,1,0:T(8,128)} %select_maximum_fusion.info_ref, bf16[2,2048,768]{2,1,0:T(8,128)(2,1)} %wg_ref.1, bf16[2,2048,768]{2,1,0:T(8,128)(2,1)} %wu_ref.1, bf16[2,768,2048]{2,1,0:T(8,128)(2,1)} %wd_ref.1), custom_call_target="tpu_custom_call" | custom-call | tf_op jit(solution)/shard_map/pallas_call | solution.py:389
  363.9 0.0 copy-start.3
  363.9 87.5 %shard_map.123 = bf16[256,2048]{1,0:T(8,128)(2,1)S(1)} custom-call(bf16[16,256,2048]{2,1,0:T(8,128)(2,1)} %shard_map.122.x_ref), custom_call_target="tpu_custom_call" | custom-call | tf_op jit(solution)/shard_map/pallas_call | solution.py:235
  451.4 0.0 copy-done.3
  451.4 1.3 add_convert_fusion
  (4 shorter events, 0.1 us)
Async XLA Ops:
  56.1 4.8 %copy-start.1 = (bf16[256,4096]{1,0:T(8,128)(2,1)S(1)}, bf16[256,4096]{1,0:T(8,128)(2,1)}, u32[]{:S(2)}) copy-start(bf16[256,4096]{1,0:T(8,128)(2,1)} %q_ref.1) | copy-start | bytes 6291460
  60.9 3.7 copy-start
  77.7 136.7 %copy-start.4 = (bf16[256,2048]{1,0:T(8,128)(2,1)S(1)}, bf16[256,2048]{1,0:T(8,128)(2,1)}, u32[]{:S(2)}) copy-start(bf16[256,2048]{1,0:T(8,128)(2,1)} %param.12) | copy-start | bytes 3145732
  222.6 1.3 copy-start.2
  363.9 87.5 %copy-start.3 = (f32[256,2048]{1,0:T(8,128)S(1)}, f32[256,2048]{1,0:T(8,128)}, u32[]{:S(2)}) copy-start(f32[256,2048]{1,0:T(8,128)} %copy-done.2) | copy-start | bytes 6291460
where the time goes:
time: 449 us; the launch traced here: 453 us
  Pallas kernels  427 us (95%)
  other arithmetic  11.2 us (2%)
  matrix products  8.27 us (2%)
  local copies, waits for them, and re-layouts  5.14 us (1%)
    pallas_call x3, Pallas kernels, ring_gather(): pl.pallas_call(functools.partial(gather_kernel, devices, pieces), out_sha...  282 us
    pallas_call x1, Pallas kernels, ring_scatter(): pl.pallas_call(functools.partial(scatter_kernel, devices, pieces), out_sh...  87.5 us
    pallas_call x1, Pallas kernels, expert_sums(): pl.pallas_call(functools.partial(expert_kernel, local, cap, per), grid=(d...  44.5 us
    pallas_call x1, Pallas kernels, attend(): pl.pallas_call(functools.partial(attend_kernel, step_rows, heads), grid=(...  13.1 us

commit v1 on v0

--- a/solution.py
+++ b/solution.py
@@ -29,7 +29,7 @@
     return place
 
 
-def gather_kernel(devices, pieces, x_ref, o_ref, local_sem, near_send, near_recv, send, recv):
+def gather_moves(devices, pieces, x_ref, o_ref, local_sem, near_send, near_recv, send, recv):
     chips = devices // 2
     me = lax.axis_index("shard")
     group = lax.axis_index("groups")
@@ -40,11 +40,6 @@
         return ring_chip(chips, (place + offset + 2 * chips) % chips) * 2 + core
 
     right, left, sibling = device_at(1), device_at(-1), me + 1 - 2 * core
-    barrier = pltpu.get_barrier_semaphore()
-    for other in (right, left, sibling):
-        pl.semaphore_signal(barrier, inc=1, device_id=(group, other), device_id_type=MESH)
-    pl.semaphore_wait(barrier, 3)
-
     rows = x_ref.shape[0] // (2 * pieces)
 
     def part(ref, way, piece):
@@ -105,43 +100,59 @@
         )
 
     every = [(way, piece) for piece in range(pieces) for way in range(2)]
-    for way, piece in every:
-        hop(0, way, piece).start()
     own = pltpu.make_async_copy(x_ref, o_ref.at[me], local_sem)
-    own.start()
-    for way, piece in every:
-        near(-1, way, piece).start()
-    for step in range(chips - 1):
+
+    def begin():
+        barrier = pltpu.get_barrier_semaphore()
+        for other in (right, left, sibling):
+            pl.semaphore_signal(barrier, inc=1, device_id=(group, other), device_id_type=MESH)
+        pl.semaphore_wait(barrier, 3)
+        for way, piece in every:
+            hop(0, way, piece).start()
+        own.start()
+        for way, piece in every:
+            near(-1, way, piece).start()
+
+    def stage(step):
         for way, piece in every:
             landing(step, way, piece).wait_recv()
             if step + 1 < chips - 1:
                 hop(step + 1, way, piece).start()
             near(step, way, piece).start()
-    own.wait()
-    for step in range(chips - 1):
-        for way, piece in every:
-            hop(step, way, piece).wait_send()
-    for step in range(-1, chips - 1):
-        for way, piece in every:
-            near(step, way, piece).wait_send()
-            near_landing(step, way, piece).wait_recv()
+
+    def finish():
+        own.wait()
+        for step in range(chips - 1):
+            for way, piece in every:
+                hop(step, way, piece).wait_send()
+        for step in range(-1, chips - 1):
+            for way, piece in every:
+                near(step, way, piece).wait_send()
+                near_landing(step, way, piece).wait_recv()
+
+    return begin, stage, finish
+
+
+def gather_kernel(devices, pieces, x_ref, o_ref, *sems):
+    begin, stage, finish = gather_moves(devices, pieces, x_ref, o_ref, *sems)
+    begin()
+    for step in range(devices // 2 - 1):
+        stage(step)
+    finish()
+
+
+def gather_scratch(devices, pieces):
+    dma = pltpu.SemaphoreType.DMA
+    return [dma] + [dma((devices // 2, 2, pieces))] * 4
 
 
 def ring_gather(x, devices, collective_id, pieces=2):
-    steps = devices // 2
-    dma = pltpu.SemaphoreType.DMA
     return pl.pallas_call(
         functools.partial(gather_kernel, devices, pieces),
         out_shape=jax.ShapeDtypeStruct((devices,) + x.shape, x.dtype),
         in_specs=[pl.BlockSpec(memory_space=pltpu.HBM)],
         out_specs=pl.BlockSpec(memory_space=pltpu.HBM),
-        scratch_shapes=[
-            dma,
-            dma((steps, 2, pieces)),
-            dma((steps, 2, pieces)),
-            dma((steps, 2, pieces)),
-            dma((steps, 2, pieces)),
-        ],
+        scratch_shapes=gather_scratch(devices, pieces),
         compiler_params=pltpu.CompilerParams(collective_id=collective_id, has_side_effects=True),
     )(x)
 
@@ -246,22 +257,36 @@
     )(x)
 
 
-def attend_kernel(step_rows, heads, count_ref, first_ref, q_ref, k_ref, v_ref, o_ref, qs, top, total):
+def attend_kernel(
+    devices, pieces, step_rows, heads, groups,
+    count_ref, q_ref, k_ref, v_ref, w_ref, o_ref, all_ref, qs, top, total, *sems
+):
+    begin, stage, finish = gather_moves(devices, pieces, w_ref, all_ref, *sems)
     rows = q_ref.shape[0]
     scale = math.log2(math.e) / math.sqrt(HD)
     count = count_ref[0]
-    first = first_ref[0]
-    seen = jnp.minimum(count, first + rows)
-    blocks = jnp.where(first < count, (seen + step_rows - 1) // step_rows, 0)
-    for h in range(heads):
-        qs[h * rows : (h + 1) * rows, :] = q_ref[:, h * HD : (h + 1) * HD]
-    top[...] = jnp.full(top.shape, NEG, jnp.float32)
-    total[...] = jnp.zeros(total.shape, jnp.float32)
-    ones = jnp.ones((step_rows, HD), jnp.bfloat16)
-
-    def fold(start, masked):
-        start = pl.multiple_of(start, step_rows)
+    first = lax.axis_index("shard") * rows
+    blocks = (first + rows + step_rows - 1) // step_rows
+    j = pl.program_id(1)
+    steps = k_ref.shape[0] // step_rows
+    at_step = pl.program_id(0) * steps + j
+    all_steps = groups * steps
+
+    @pl.when(at_step == 0)
+    def _():
+        begin()
+
+    @pl.when(j == 0)
+    def _():
+        for h in range(heads):
+            qs[h * rows : (h + 1) * rows, :] = q_ref[:, h * HD : (h + 1) * HD]
+        top[...] = jnp.full(top.shape, NEG, jnp.float32)
+        total[...] = jnp.zeros(total.shape, jnp.float32)
+
+    def fold(masked):
+        start = pl.multiple_of(j * step_rows, step_rows)
         keys = k_ref[pl.ds(start, step_rows), :]
+        ones = jnp.ones((step_rows, HD), jnp.bfloat16)
         values = jnp.concatenate([v_ref[pl.ds(start, step_rows), :], ones], axis=1)
         if masked:
             at_row = first + lax.broadcasted_iota(jnp.int32, (rows, step_rows), 0)
@@ -282,51 +307,63 @@
             total[span, :] = total[span, :] * jnp.concatenate([factor, factor], axis=1) + part
             top[span, :] = new
 
-    def body(i, carry):
-        fold(i * step_rows, False)
-        return carry
-
-    lax.fori_loop(0, blocks - 1, body, 0)
-
-    @pl.when(blocks > 0)
-    def _():
-        fold((blocks - 1) * step_rows, True)
-
-    live = first + lax.broadcasted_iota(jnp.int32, (rows, HD), 0) < count
-    for h in range(heads):
-        both = total[h * rows : (h + 1) * rows, :]
-        result = jnp.where(live, both[:, :HD] / jnp.where(live, both[:, HD:], 1.0), 0.0)
-        o_ref[:, h * HD : (h + 1) * HD] = result.astype(jnp.bfloat16)
-
-
-def attend(count, first, queries, keys_values, kv_count):
+    @pl.when(j < blocks - 1)
+    def _():
+        fold(False)
+
+    @pl.when(j == blocks - 1)
+    def _():
+        fold(True)
+
+        live = first + lax.broadcasted_iota(jnp.int32, (rows, HD), 0) < count
+        for h in range(heads):
+            both = total[h * rows : (h + 1) * rows, :]
+            result = jnp.where(live, both[:, :HD] / jnp.where(live, both[:, HD:], 1.0), 0.0)
+            o_ref[:, h * HD : (h + 1) * HD] = result.astype(jnp.bfloat16)
+
+    stages = devices // 2 - 1
+    for number in range(stages):
+
+        @pl.when(at_step == (number + 1) * all_steps // stages - 1)
+        def _(number=number):
+            stage(number)
+
+    @pl.when(at_step == all_steps - 1)
+    def _():
+        finish()
+
+
+def attend(count, queries, keys_values, out_weight, kv_count, devices, collective_id, pieces=2):
     rows, width = queries.shape
     length = keys_values.shape[0]
     heads = width // HD // kv_count
     step_rows = math.gcd(length, 512)
-    smem = pl.BlockSpec(memory_space=pltpu.SMEM)
+    hbm = pl.BlockSpec(memory_space=pltpu.HBM)
     return pl.pallas_call(
-        functools.partial(attend_kernel, step_rows, heads),
-        grid=(kv_count,),
-        out_shape=jax.ShapeDtypeStruct((rows, width), jnp.bfloat16),
+        functools.partial(attend_kernel, devices, pieces, step_rows, heads, kv_count),
+        grid=(kv_count, length // step_rows),
+        out_shape=(
+            jax.ShapeDtypeStruct((rows, width), jnp.bfloat16),
+            jax.ShapeDtypeStruct((devices,) + out_weight.shape, jnp.bfloat16),
+        ),
         in_specs=[
-            smem,
-            smem,
-            pl.BlockSpec((rows, heads * HD), lambda g: (0, g)),
-            pl.BlockSpec((length, HD), lambda g: (0, g)),
-            pl.BlockSpec((length, HD), lambda g: (0, kv_count + g)),
+            pl.BlockSpec(memory_space=pltpu.SMEM),
+            pl.BlockSpec((rows, heads * HD), lambda g, j: (0, g)),
+            pl.BlockSpec((length, HD), lambda g, j: (0, g)),
+            pl.BlockSpec((length, HD), lambda g, j: (0, kv_count + g)),
+            hbm,
         ],
-        out_specs=pl.BlockSpec((rows, heads * HD), lambda g: (0, g)),
+        out_specs=(pl.BlockSpec((rows, heads * HD), lambda g, j: (0, g)), hbm),
         scratch_shapes=[
             pltpu.VMEM((heads * rows, HD), jnp.bfloat16),
             pltpu.VMEM((heads * rows, HD), jnp.float32),
             pltpu.VMEM((heads * rows, 2 * HD), jnp.float32),
-        ],
-        compiler_params=pltpu.CompilerParams(vmem_limit_bytes=40 << 20),
-        cost_estimate=pl.CostEstimate(
-            flops=4 * rows * width * length, bytes_accessed=12 << 20, transcendentals=rows * width * length // HD
+        ]
+        + gather_scratch(devices, pieces),
+        compiler_params=pltpu.CompilerParams(
+            collective_id=collective_id, has_side_effects=True, vmem_limit_bytes=40 << 20
         ),
-    )(count, first, queries, keys_values, keys_values)
+    )(count, queries, keys_values, keys_values, out_weight)
 
 
 def expert_kernel(local, cap, per, count_ref, x_ref, info_ref, wg_ref, wu_ref, wd_ref, o_ref, picked, given):
@@ -447,9 +484,10 @@
     info = jnp.pad(info, ((0, 0), (0, -info.shape[1] % 8), (0, 0)))
 
     both = both.reshape(devices * tok_dev, both.shape[2])
-    first = (me * tok_dev).astype(jnp.int32).reshape(1)
-    attended = attend(counts, first, query_rows, both, key_rows.shape[1] // HD)
-    out_all = ring_gather(out_weight, devices, 1).reshape(-1, depth)
+    attended, out_all = attend(
+        counts, query_rows, both, out_weight, key_rows.shape[1] // HD, devices, 1
+    )
+    out_all = out_all.reshape(-1, depth)
     mixed_rows = hidden.astype(jnp.float32) + jnp.dot(
         attended, out_all, preferred_element_type=jnp.float32
     )

time: 449 us -> 380 us (0.85)
  the two profiles are of different devices: /device:TPU:3 before, /device:TPU:13 now
where the time goes in v1:
time: 380 us; the launch traced here: 374 us
  Pallas kernels  354 us (93%)
  other arithmetic  11.2 us (3%)
  matrix products  8.26 us (2%)
    pallas_call x2, Pallas kernels, ring_gather(): pl.pallas_call(functools.partial(gather_kernel, devices, pieces), out_sha...  142 us
    pallas_call x1, Pallas kernels, attend(): pl.pallas_call(functools.partial(attend_kernel, devices, pieces, step_row...  89.4 us
    pallas_call x1, Pallas kernels, ring_scatter(): pl.pallas_call(functools.partial(scatter_kernel, devices, pieces), out_sh...  84.8 us
    pallas_call x1, Pallas kernels, expert_sums(): pl.pallas_call(functools.partial(expert_kernel, local, cap, per), grid=(d...  37.1 us
    dot_general x1, matrix products, per_device(): jnp.dot(attended, out_all, preferred_element_type=jnp.float32)  8.26 us

profile of v1, /device:TPU:13, one launch (start us, length us, event | category | flops | bytes accessed | tf_op | source)
XLA Modules:
  0.0 373.9 jit_solution(4135715561109943950)
XLA Ops:
  0.7 0.7 convert_element_type.36
  1.4 0.7 pad_maximum_fusion
  2.0 0.7 convert_element_type.37
  2.7 0.1 copy.15
  2.9 1.9 fusion.3.x_ref
  4.7 0.0 copy-start.1
  4.7 51.4 %shard_map.118 = bf16[16,256,1152]{2,1,0:T(8,128)(2,1)} custom-call(bf16[256,1152]{1,0:T(8,128)(2,1)} %fusion.3.x_ref), custom_call_target="tpu_custom_call" | custom-call | tf_op jit(solution)/shard_map/pallas_call | solution.py:150
  56.1 0.0 copy-start
  56.1 4.0 %convert_reduce_fusion.1 = (f32[16,256]{1,0:T(8,128)S(1)}, f32[16,256]{1,0:T(8,128)S(1)}, f32[16,256]{1,0:T(8,128)S(1)}, f32[16,256]{1,0:T(8,128)S(1)}) fusion(s32[]{:T(128)S(6)} %mul.30, bf16[16,256,1152]{2,1,0:T(8,128)(2,1)} %shard_map.118, s32[]{:T(128)S(6)} %add.40), kind=kLoop, calls=%fused_computation.9 | loop fusion | flops 376832 | bytes 196616 | tf_op jit(solution)/shard_map/reduce_sum | solution.py:479
  60.2 0.7 select_maximum_fusion.info_ref
  60.9 0.0 copy-done.1
  60.9 0.0 copy-done
  60.9 0.0 copy-start.2
  60.9 89.4 %shard_map.119 = (bf16[256,4096]{1,0:T(8,128)(2,1)S(1)}, bf16[16,256,2048]{2,1,0:T(8,128)(2,1)}) custom-call(s32[1]{0:T(128)} %copy.16.count_ref, bf16[256,4096]{1,0:T(8,128)(2,1)S(1)} %copy-done, bf16[4096,1152]{1,0:T(8,128)(2,1)} %bitcast.6, bf16[4096,1152]{1,0:T(8,128)(2,1)} %bitcast.7, bf16[256,2048]{1,0:T(8,128)(2,1)S(1)} %copy-done.1), custom_call_target="tpu_custom_call" | custom-call | tf_op jit(solution)/shard_map/pallas_call | solution.py:342
  150.3 0.0 copy-done.2
  150.3 8.3 %multiply_reduce_fusion = (f32[256]{0:T(256)S(1)}, f32[256,2048]{1,0:T(8,128)S(1)}) fusion(bf16[256,4096]{1,0:T(8,128)(2,1)S(1)} %get-tuple-element.7, bf16[4096,2048]{1,0:T(8,128)(2,1)} %bitcast.8, bf16[256,2048]{1,0:T(8,128)(2,1)S(1)} %copy-done.2), kind=kOutput, calls=%fused_computation.11 | convolution fusion | flops 4297064448 | bytes 22021120 | tf_op jit(solution)/shard_map/dot_general | solution.py:491
  158.6 1.2 multiply_convert_fusion.x_ref
  159.8 91.0 %shard_map.120.x_ref = bf16[16,256,2048]{2,1,0:T(8,128)(2,1)} custom-call(bf16[256,2048]{1,0:T(8,128)(2,1)} %multiply_convert_fusion.x_ref), custom_call_target="tpu_custom_call" | custom-call | tf_op jit(solution)/shard_map/pallas_call | solution.py:150
  250.8 37.1 %shard_map.121.x_ref = bf16[16,256,2048]{2,1,0:T(8,128)(2,1)} custom-call(s32[1]{0:T(128)} %copy.16.count_ref, bf16[16,256,2048]{2,1,0:T(8,128)(2,1)} %shard_map.120.x_ref, f32[16,8,256]{2,1,0:T(8,128)} %select_maximum_fusion.info_ref, bf16[2,2048,768]{2,1,0:T(8,128)(2,1)} %wg_ref.1, bf16[2,2048,768]{2,1,0:T(8,128)(2,1)} %wu_ref.1, bf16[2,768,2048]{2,1,0:T(8,128)(2,1)} %wd_ref.1), custom_call_target="tpu_custom_call" | custom-call | tf_op jit(solution)/shard_map/pallas_call | solution.py:426
  287.9 84.8 %shard_map.122 = bf16[256,2048]{1,0:T(8,128)(2,1)S(1)} custom-call(bf16[16,256,2048]{2,1,0:T(8,128)(2,1)} %shard_map.121.x_ref), custom_call_target="tpu_custom_call" | custom-call | tf_op jit(solution)/shard_map/pallas_call | solution.py:246
  372.7 1.3 add_convert_fusion
  (4 shorter events, 0.1 us)
Async XLA Ops:
  4.7 56.2 %copy-start.1 = (bf16[256,2048]{1,0:T(8,128)(2,1)S(1)}, bf16[256,2048]{1,0:T(8,128)(2,1)}, u32[]{:S(2)}) copy-start(bf16[256,2048]{1,0:T(8,128)(2,1)} %w_ref.1) | copy-start | bytes 3145732
  56.1 4.8 %copy-start = (bf16[256,4096]{1,0:T(8,128)(2,1)S(1)}, bf16[256,4096]{1,0:T(8,128)(2,1)}, u32[]{:S(2)}) copy-start(bf16[256,4096]{1,0:T(8,128)(2,1)} %q_ref.1) | copy-start | bytes 6291460
  60.9 89.4 %copy-start.2 = (bf16[256,2048]{1,0:T(8,128)(2,1)S(1)}, bf16[256,2048]{1,0:T(8,128)(2,1)}, u32[]{:S(2)}) copy-start(bf16[256,2048]{1,0:T(8,128)(2,1)} %param.12) | copy-start | bytes 3145732
